TPU v7x, 512 devices: a whole 4x8x8 slice. The times are simulated.
512 devices in a mesh: seq: 128 (over x, z, y_hi, core), head: 4 (over y_lo).
Axes of the slice: x: 4, y: 8 (y_hi: 2, y_lo: 4; y = y_hi * 4 + y_lo), z: 8, core: 2. Of those that a mesh axis runs over, the one named last changes fastest.
Arguments:
- queries: bfloat16 [16384, 512], P('seq'), may hold values from -52 to 52
- source: bfloat16 [16384, 512], P('seq'), may hold values from -6 to 6
- order: int32 [16384], P('seq'), may hold values from 0 to 127, as said below
- avail: int32 [16384], P('seq'), may hold values from 0 to 1, as said below
- pos_table: bfloat16 [16384, 2, 512], P('seq', None, 'head'), may hold values from -6 to 6
- w_query: bfloat16 [512, 512], P(None, 'head'), may hold values from -0.25 to 0.25
- w_keyval: bfloat16 [512, 2, 512], P(None, None, 'head'), may hold values from -0.25 to 0.25
- w_out: bfloat16 [512, 512], P('head'), may hold values from -0.25 to 0.25
Outputs:
- joined: bfloat16 [16384, 512], P('seq', 'head')
Inputs may be any that keep to these rules, and one draw needn't show every extreme that they name: `order`: each aligned block of 128 entries is a permutation of 0 to 127. `avail`: every aligned block of 8 entries holds at least one 1.
All inputs are finite; a program needn't handle non-finite values.
Results may differ from a plain program's by a relative error of at most 0.0085.
Values may be sent and summed in bfloat16 or wider, within the bound.
No kernel may reach another device: no remote copies, remote signals or barrier semaphores. Data moves between devices by JAX's collectives and lax.ppermute only.
A program may use at most 128 MiB of HBM per device.

v0:
```python
import math

import jax
import jax.numpy as jnp
from jax import lax
from jax.sharding import PartitionSpec as P

HEADS = 8
HD = 64


def side_by_side(arrays, axis, dim, along):
    widths = [math.prod(a.shape[along:]) for a in arrays]
    both = jnp.concatenate(
        [a.reshape(*a.shape[:along], w) for a, w in zip(arrays, widths)], axis=along
    )
    whole = lax.all_gather(both, axis, axis=dim, tiled=True)
    parts = jnp.split(whole, [sum(widths[:k]) for k in range(1, len(widths))], axis=along)
    return tuple((b.reshape(*whole.shape[:along], *a.shape[along:]) for a, b in zip(arrays, parts)))


def cut_along(array, dim, peers):
    before, after = (array.shape[:dim], array.shape[dim + 1 :])
    return jnp.moveaxis(array.reshape(*before, peers, -1, *after), dim, 0)


def sum_at_owner(array, axis, dim):
    parts = cut_along(array, dim, lax.axis_size(axis))
    arrived = lax.all_to_all(parts, axis, split_axis=0, concat_axis=0, tiled=True)
    return arrived.astype(jnp.float32).sum(axis=0)


def attend_block(carry, keyval, flags, query, scale):
    high, total, summed = carry
    count = keyval.shape[0]
    heads = query.shape[1]
    keys = keyval[:, 0].reshape(count, heads, -1)
    values = keyval[:, 1].reshape(count, heads, -1)
    score = jnp.einsum("qhe,khe->hqk", query, keys, preferred_element_type=jnp.float32) * scale
    live = (flags > 0)[None, None, :]
    score = jnp.where(live, score, jnp.float32(-1e30))
    newest = jnp.maximum(high, jnp.max(score, axis=-1))
    weight = jnp.where(live, jnp.exp(score - newest[..., None]), jnp.float32(0.0))
    factor = jnp.exp(high - newest)
    total = total * factor + jnp.sum(weight, axis=-1)
    summed = summed * factor[..., None] + jnp.einsum(
        "hqk,khe->hqe", weight.astype(jnp.bfloat16), values, preferred_element_type=jnp.float32
    )
    return (newest, total, summed)


def local(queries, source, order, avail, pos_table, w_query, w_keyval, w_out):
    qrows = queries.shape[0]
    cols = w_query.shape[1]
    heads = HEADS // lax.axis_size("head")
    head_size = cols // heads
    scale = 2.0 / HD**0.5
    sectioned = jnp.take(source, order, axis=0)
    sectioned_flags = jnp.take(avail, order, axis=0).astype(jnp.bfloat16)
    positions = lax.all_to_all(pos_table, "seq", split_axis=0, concat_axis=0, tiled=True)
    proj = jnp.einsum("rd,djc->rjc", sectioned, w_keyval, preferred_element_type=jnp.float32)
    keyval = (proj + positions.astype(jnp.float32)).astype(jnp.bfloat16)
    query = jnp.dot(queries, w_query, preferred_element_type=jnp.float32).astype(jnp.bfloat16)
    query = query.reshape(qrows, heads, head_size)
    start_high = jnp.full((heads, qrows), -1e30, jnp.float32)
    start_total = jnp.zeros((heads, qrows), jnp.float32)
    start_sum = jnp.zeros((heads, qrows, head_size), jnp.float32)
    tile_kv, tile_flags = side_by_side((keyval, sectioned_flags), "seq", 0, 1)
    count = tile_kv.shape[0]
    blocked_kv = tile_kv.reshape((count // 512, 512) + tile_kv.shape[1:])
    blocked_flags = tile_flags.reshape(count // 512, 512)

    def step(inner, items):
        return (attend_block(inner, items[0], items[1], query, scale), None)

    result, unused = lax.scan(
        step, (start_high, start_total, start_sum), (blocked_kv, blocked_flags)
    )
    high, total, summed = result
    result = summed / total[..., None]
    attn = jnp.transpose(result, (1, 0, 2)).reshape(qrows, cols).astype(jnp.bfloat16)
    own_cols = lax.dynamic_slice_in_dim(queries, lax.axis_index("head") * cols, cols, 1).astype(
        jnp.float32
    )
    terms = jnp.dot(attn, w_out, preferred_element_type=jnp.float32)
    mixed = sum_at_owner(terms.astype(jnp.bfloat16), "head", 1)
    return (own_cols + mixed).astype(jnp.bfloat16)


def solution(mesh):
    in_specs = (
        P("seq", None),
        P("seq", None),
        P("seq"),
        P("seq"),
        P("seq", None, "head"),
        P(None, "head"),
        P(None, None, "head"),
        P("head", None),
    )
    out_specs = P("seq", "head")
    return jax.shard_map(local, mesh=mesh, in_specs=in_specs, out_specs=out_specs, check_vma=False)
```

profile of v0, /device:TPU:4, one launch (start us, length us, event | category | flops | bytes accessed | tf_op | source)
XLA Modules:
  0.0 267.0 jit_solution(3082517355266499172)
XLA Ops:
  6.5 20.3 %all-to-all-start = ((bf16[128,2,128]{2,1,0:T(2,128)(2,1)}), bf16[128,2,128]{2,1,0:T(2,128)(2,1)S(1)}, u32[]{:S(2)}, u32[]{:S(2)}) async-start(bf16[128,2,128]{2,1,0:T(2,128)(2,1)} %param.14), calls=%async_computation | async-start | bytes 131072 | tf_op jit(solution)/shard_map/all_to_all | solution.py:60
  27.6 1.6 gather_fusion.1
  29.8 1.1 copy.17
  32.1 7.4 %all-to-all-done = bf16[128,2,128]{2,1,0:T(2,128)(2,1)S(1)} async-done(((bf16[128,2,128]{2,1,0:T(2,128)(2,1)}), bf16[128,2,128]{2,1,0:T(2,128)(2,1)S(1)}, u32[]{:S(2)}, u32[]{:S(2)}) %all-to-all-start) | async-done | bytes 65568 | tf_op jit(solution)/shard_map/all_to_all | solution.py:60
  40.3 1.2 convolution_convert_fusion.1
  41.5 115.9 %all-gather.2.cloned.1.call-done = bf16[16384,257]{0,1:T(8,128)(2,1)} async-done(((bf16[128,257]{0,1:T(8,128)(2,1)}), bf16[16384,257]{0,1:T(8,128)(2,1)}) %all-gather.2.cloned.1.call-update) | async-done | bytes 8421392 | tf_op jit(solution)/shard_map/all_gather | solution.py:17
  157.5 1.1 slice_reduce_fusion
  158.6 7.5 %split.9 = bf16[16384,256]{0,1:T(8,128)(2,1)} slice(bf16[16384,257]{0,1:T(8,128)(2,1)} %all-gather.2.cloned.1.call-done), slice={[0:16384], [0:256]} | slice | bytes 16777216 | tf_op jit(solution)/shard_map/split | solution.py:18
  166.1 10.4 %copy.23 = bf16[32,8,32,512]{3,2,1,0:T(8,128)(2,1)} copy(bf16[32,8,32,512]{3,1,2,0:T(8,128)(2,1)} %bitcast.48) | data formatting | bytes 16777216
  176.5 11.3 %copy.19 = bf16[32,512,2,128]{1,3,2,0:T(8,128)(2,1)} copy(bf16[32,512,2,128]{1,0,3,2:T(8,128)(2,1)} %bitcast.49) | data formatting | bytes 16777216
  187.9 59.0 %while.15 = (s32[]{:T(128)}, f32[2,128]{1,0:T(2,128)S(1)}, f32[2,128]{1,0:T(2,128)S(1)}, f32[2,128,64]{1,2,0:T(8,128)S(1)}, bf16[32,512]{1,0:T(8,128)(2,1)S(1)},...) while((s32[]{:T(128)}, f32[2,128]{1,0:T(2,128)S(1)}, ...), condition=%wide.region_3.4_spmd.clone, body=%wide.region_0.3_spmd.clone.sunk | while | flops 34786048 | bytes 3067001 | solution.py:76
  187.9 1.0 dynamic-slice_bitcast_fusion.2
  189.7 1.0 dynamic-slice_bitcast_fusion.2
  191.6 1.0 dynamic-slice_bitcast_fusion.2
  193.4 1.0 dynamic-slice_bitcast_fusion.2
  195.3 1.0 dynamic-slice_bitcast_fusion.2
  197.1 1.0 dynamic-slice_bitcast_fusion.2
  199.0 1.0 dynamic-slice_bitcast_fusion.2
  200.8 1.0 dynamic-slice_bitcast_fusion.2
  202.7 1.0 dynamic-slice_bitcast_fusion.2
  204.5 1.0 dynamic-slice_bitcast_fusion.2
  247.8 4.6 %all-to-all-start.1 = ((bf16[4,128,128]{2,1,0:T(8,128)(2,1)}), bf16[4,128,128]{2,1,0:T(8,128)(2,1)S(1)}, u32[]{:S(2)}, u32[]{:S(2)}) async-start(bf16[4,128,128]{2,1,0:T(8,128)(2,1)} %bitcast.35), calls=%async_computation.1 | async-start | bytes 262144 | tf_op jit(solution)/shard_map/all_to_all | solution.py:29
  252.4 6.3 %all-to-all-done.1 = bf16[4,128,128]{2,1,0:T(8,128)(2,1)S(1)} async-done(((bf16[4,128,128]{2,1,0:T(8,128)(2,1)}), bf16[4,128,128]{2,1,0:T(8,128)(2,1)S(1)}, u32[]{:S(2)}, u32[]{:S(2)}) %all-to-all-start.1) | async-done | bytes 131104 | tf_op jit(solution)/shard_map/all_to_all | solution.py:29
  258.8 1.4 add_convert_fusion.1
  (300 shorter events, 51.9 us)
Async XLA Ops:
  6.5 24.4 %copy-start = (bf16[128,512]{1,0:T(8,128)(2,1)S(1)}, bf16[128,512]{1,0:T(8,128)(2,1)}, u32[]{:S(2)}) copy-start(bf16[128,512]{1,0:T(8,128)(2,1)} %param.11) | copy-start | bytes 393220
  6.5 33.0 %all-to-all-start = ((bf16[128,2,128]{2,1,0:T(2,128)(2,1)}), bf16[128,2,128]{2,1,0:T(2,128)(2,1)S(1)}, u32[]{:S(2)}, u32[]{:S(2)}) async-start(bf16[128,2,128]{2,1,0:T(2,128)(2,1)} %param.14), calls=%async_computation | async-start | bytes 131072 | tf_op jit(solution)/shard_map/all_to_all | solution.py:60
  26.9 130.6 %all-gather.2.cloned.1.call-start = ((), (), s32[]{:S(2)}) async-start(), calls=%async_computation.2 | async-start | bytes 8718336 | tf_op jit(solution)/shard_map/all_gather | solution.py:17
  187.9 59.1 %copy-start.1 = (bf16[128,512]{1,0:T(8,128)(2,1)S(1)}, bf16[128,512]{1,0:T(8,128)(2,1)}, u32[]{:S(2)}) copy-start(bf16[128,512]{1,0:T(8,128)(2,1)} %param.17) | copy-start | bytes 393220
  247.8 10.9 %all-to-all-start.1 = ((bf16[4,128,128]{2,1,0:T(8,128)(2,1)}), bf16[4,128,128]{2,1,0:T(8,128)(2,1)S(1)}, u32[]{:S(2)}, u32[]{:S(2)}) async-start(bf16[4,128,128]{2,1,0:T(8,128)(2,1)} %bitcast.35), calls=%async_computation.1 | async-start | bytes 262144 | tf_op jit(solution)/shard_map/all_to_all | solution.py:29
Sparse Core Ops, SparseCore 0:
  40.4 117.0 all-gather.1
where the time goes:
time: 269 us; the launch traced here: 267 us
  waiting for transfers between devices  130 us (48%)
  local copies, waits for them, and re-layouts  66.5 us (25%)
  starting transfers between devices  25 us (9%)
  matrix products  20.7 us (8%)
  between operations  13.5 us (5%)
  other arithmetic  9.94 us (4%)
    all_gather x1, waiting for transfers between devices, side_by_side(): whole = lax.all_gather(both, axis, axis=dim, tiled=True)  116 us
    squeeze x32, local copies, waits for them, and re-layouts, local(): lax.scan(step, (start_high, start_total, start_sum), (blocked_kv, blocked...  31.1 us
    unnamed x7, local copies, waits for them, and re-layouts  22.9 us
    all_to_all x1, starting transfers between devices, local(): lax.all_to_all(pos_table, 'seq', split_axis=0, concat_axis=0, tiled=True)  20.3 us
    dot_general x32, matrix products, attend_block(): jnp.einsum('hqk,khe->hqe', weight.astype(jnp.bfloat16), values, preferred...  9.6 us
    dot_general x32, matrix products, attend_block(): jnp.einsum('qhe,khe->hqk', query, keys, preferred_element_type=jnp.float32)  9.43 us
    split x2, local copies, waits for them, and re-layouts, side_by_side(): jnp.split(whole, [sum(widths[:k]) for k in range(1, len(widths))], axis=a...  8.62 us
    all_to_all x1, waiting for transfers between devices, local(): lax.all_to_all(pos_table, 'seq', split_axis=0, concat_axis=0, tiled=True)  7.36 us
  transfers between devices with their start and end apart: 3, of which 3 were waited for; matrix products, arithmetic and copies ran while one was open for 2% of the time, Pallas kernels for 0%

commit v1 on v0

v1 whole, which is shorter than its diff:
```python
import functools

import jax
import jax.numpy as jnp
from jax import lax
from jax.experimental import pallas as pl
from jax.experimental.pallas import tpu as pltpu
from jax.sharding import Mesh
from jax.sharding import PartitionSpec as P

HD = 64
SPLIT = (("x", 4), ("zh", 4), ("zl", 2), ("yh", 2), ("c", 2))
SEQ = tuple(n for n, _ in SPLIT)
I = ("zh", "yh")
J = ("x", "zl")
NI = 8
NJ = 8
BIG = 1048576.0
CUT = 65536.0
NEG = -1e30
F32 = jnp.float32
BF16 = jnp.bfloat16


def seq_of(i, j, c):
    size = dict(SPLIT)
    part = {"c": c}
    for names, index in ((I, i), (J, j)):
        for name in reversed(names):
            part[name] = index % size[name]
            index = index // size[name]
    place = 0
    for name, n in SPLIT:
        place = place * n + part[name]
    return place


def iota(shape, dim):
    return lax.broadcasted_iota(jnp.int32, shape, dim)


def onehot(mask):
    return jnp.where(mask, F32(1.0), F32(0.0)).astype(BF16)


def mm(a, b, ca=1, cb=0):
    return lax.dot_general(a, b, (((ca,), (cb,)), ((), ())), preferred_element_type=F32)


def split_kernel(pos_ref, out_ref):
    row, col = iota((128, 128), 0), iota((128, 128), 1)
    relay = onehot(col == seq_of(row // 16, row % 8, (row // 8) % 2))
    for part in range(2):
        out_ref[:, part * 8 : part * 8 + 8, :] = (
            mm(relay, pos_ref[:, part, :]).astype(BF16).reshape(2 * NI, NJ, 128)
        )


def pack_kernel(source_ref, order_ref, avail_ref, queries_ref, wq_ref, out_ref):
    row, col = iota((128, 128), 0), iota((128, 128), 1)
    pick = onehot(jnp.broadcast_to(order_ref[...], (128, 128)) == row)
    relay = onehot(row == seq_of((col // 2) % NI, col // 16, col % 2))
    pick = mm(pick, relay).astype(BF16)
    avail = jnp.broadcast_to(avail_ref[...], (128, 128))
    diag = onehot((row == col) & (avail > 0))
    flags = mm(diag, jnp.ones((128, 512), BF16)).astype(BF16)
    live = mm(pick, flags, 0, 0) > 0.5
    rows = jnp.where(live, mm(pick, source_ref[...], 0, 0), F32(BIG)).astype(BF16)
    q = mm(queries_ref[...], wq_ref[...]).astype(BF16)
    q = (q.astype(F32) * (2.0 / HD**0.5)).astype(BF16)
    for j in range(NJ):
        for part in range(4):
            out_ref[j, part * 16 : part * 16 + 16, :] = rows[
                j * 16 : j * 16 + 16, part * 128 : part * 128 + 128
            ]
        out_ref[j, 64:192, :] = q


def project_kernel(got_ref, pos_ref, wk_ref, wv_ref, out_ref):
    parts = [got_ref[:, part * 16 : part * 16 + 16, :].reshape(128, 128) for part in range(4)]
    live = parts[0].astype(F32) < CUT
    rows = jnp.concatenate(parts, axis=1)
    row, col = iota((128, 128), 0), iota((128, 128), 1)
    relay = onehot(col == (row % 16) * 8 + row // 16)
    for part, w_ref, mark in ((0, wk_ref, BIG), (1, wv_ref, 0.0)):
        pos = pos_ref[:, part * 8 : part * 8 + 8, :].reshape(128, 128)
        out = mm(rows, w_ref[...]) + mm(relay, pos)
        out = jnp.where(live, out, F32(mark)).astype(BF16)
        for i in range(NI):
            out_ref[i, part] = out


def attend_kernel(got_ref, own_ref, other_ref, out_ref, kaug_ref, vaug_ref, *, qb):
    n = NI * 128
    lane = iota((n, 128), 1)
    for side, ref in ((0, own_ref), (1, other_ref)):
        keys = ref[:, 0].reshape(n, 128).astype(F32)
        values = ref[:, 1].reshape(n, 128).astype(F32)
        bad = keys > CUT
        for h in range(2):
            mark = lane == 64 * (1 - h)
            kaug_ref[h, side * n : side * n + n] = jnp.where(
                mark, jnp.where(bad, F32(NEG), F32(0.0)), jnp.where(bad, F32(0.0), keys)
            ).astype(BF16)
            mine = (lane >= 64) if h else (lane < 64)
            vaug_ref[h, side * n : side * n + n] = jnp.where(mine, values, F32(1.0)).astype(BF16)

    lane = iota((qb, 128), 1)
    erow, ecol = iota((16, 128), 0), iota((16, 128), 1)
    pull = onehot((erow < 6) & (ecol == erow % 3 + 64 * (erow // 3)))
    per = qb // 128

    def block(t, carry):
        q = got_ref[pl.ds(t * per, per), 64:192, :].reshape(qb, 128).astype(F32)
        sums, tops = [], []
        for h in range(2):
            mine = (lane >= 64) if h else (lane < 64)
            qh = jnp.where(mine, q, jnp.where(lane == 64 * (1 - h), F32(1.0), F32(0.0)))
            score = mm(qh.astype(BF16), kaug_ref[h], 1, 1)
            top = jnp.max(score, axis=1, keepdims=True)
            weight = jnp.exp(score - top).astype(BF16)
            sums.append(mm(weight, vaug_ref[h]))
            tops.append(top)
        low = lane < 64
        summed = jnp.where(low, sums[0], sums[1])
        total = pltpu.roll(jnp.where(low, sums[1], sums[0]), 64, 1)
        mean = (summed / total).astype(BF16)
        lse = jnp.where(low, tops[0], tops[1]) + jnp.log(total)
        hi = lse.astype(BF16).astype(F32)
        mid = (lse - hi).astype(BF16).astype(F32)
        tail = lse - hi - mid
        which = lane % 64
        piece = jnp.where(which == 0, hi, jnp.where(which == 1, mid, tail)).astype(BF16)
        for u in range(per):
            out_ref[t * per + u, 0:128, :] = mean[u * 128 : u * 128 + 128]
            out_ref[t * per + u, 128:144, :] = mm(pull, piece[u * 128 : u * 128 + 128], 1, 1).astype(BF16)
        return carry

    lax.fori_loop(0, NJ // per, block, 0)


def combine_kernel(got_ref, wo_ref, out_ref):
    row, col = iota((16, 128), 0), iota((16, 128), 1)
    push = onehot(((row < 3) & (col < 64)) | ((row >= 3) & (row < 6) & (col >= 64)))
    lse = [mm(got_ref[j, 128:144, :], push, 0, 0) for j in range(NJ)]
    top = functools.reduce(jnp.maximum, lse)
    total = jnp.zeros((128, 128), F32)
    summed = jnp.zeros((128, 128), F32)
    for j in range(NJ):
        w = jnp.exp(lse[j] - top)
        total = total + w
        summed = summed + w * got_ref[j, 0:128, :].astype(F32)
    attn = (summed / total).astype(BF16)
    terms = mm(attn, wo_ref[...]).astype(BF16)
    for h in range(4):
        out_ref[h] = terms[:, h * 128 : h * 128 + 128]


def vcall(kernel, out, args, scalars=0, scratch=()):
    specs = [pl.BlockSpec(memory_space=pltpu.SMEM)] * scalars
    specs += [pl.BlockSpec(memory_space=pltpu.VMEM)] * (len(args) - scalars)
    outs = jax.tree.map(lambda _: pl.BlockSpec(memory_space=pltpu.VMEM), out)
    return pl.pallas_call(
        kernel,
        out_shape=out,
        in_specs=specs,
        out_specs=outs,
        scratch_shapes=list(scratch),
        compiler_params=pltpu.CompilerParams(vmem_limit_bytes=48 * 1024 * 1024),
    )(*args)


def bf(*shape):
    return jax.ShapeDtypeStruct(shape, BF16)


def swap(x, axes):
    return lax.all_to_all(x, axes, split_axis=0, concat_axis=0, tiled=True)


def local(queries, source, order, avail, pos_table, w_query, w_keyval, w_out):
    pos = swap(vcall(split_kernel, bf(2 * NI, 16, 128), (pos_table,)), (*I, "c"))
    packed = vcall(
        pack_kernel,
        bf(NJ, 192, 128),
        (source, order.reshape(1, 128), avail.reshape(1, 128), queries, w_query),
    )
    got = swap(packed, J)
    spread = vcall(
        project_kernel, bf(NI, 2, 128, 128), (got, pos, w_keyval[:, 0], w_keyval[:, 1])
    )
    own = swap(spread, I)
    other = lax.ppermute(own, "c", ((0, 1), (1, 0)))
    partial = vcall(
        functools.partial(attend_kernel, qb=256),
        bf(NJ, 144, 128),
        (got, own, other),
        scratch=(pltpu.VMEM((2, 2048, 128), BF16), pltpu.VMEM((2, 2048, 128), BF16)),
    )
    partial = swap(partial, J)
    terms = vcall(combine_kernel, bf(4, 128, 128), (partial, w_out))
    terms = swap(terms, "head")
    own = lax.dynamic_slice_in_dim(queries, lax.axis_index("head") * 128, 128, 1)
    return (own.astype(F32) + terms.astype(F32).sum(axis=0)).astype(BF16)


def solution(mesh):
    fine = Mesh(mesh.devices.reshape(*(n for _, n in SPLIT), 4), (*SEQ, "head"))
    in_specs = (
        P(SEQ, None),
        P(SEQ, None),
        P(SEQ),
        P(SEQ),
        P(SEQ, None, "head"),
        P(None, "head"),
        P(None, None, "head"),
        P("head", None),
    )
    out_specs = P(SEQ, "head")
    return jax.shard_map(local, mesh=fine, in_specs=in_specs, out_specs=out_specs, check_vma=False)
```

time: 269 us -> 101 us (0.38)
  the two profiles are of different devices: /device:TPU:4 before, /device:TPU:8 now
where the time goes in v1:
time: 101 us; the launch traced here: 100 us
  blocking collectives  34.5 us (34%)
  waiting for transfers between devices  25.6 us (25%)
  starting transfers between devices  25.2 us (25%)
  Pallas kernels  11.3 us (11%)
  local copies, waits for them, and re-layouts  2.84 us (3%)
    all_to_all x2, blocking collectives, swap(): return lax.all_to_all(x, axes, split_axis=0, concat_axis=0, tiled=True)  34.5 us
    all_to_all x3, waiting for transfers between devices, swap(): return lax.all_to_all(x, axes, split_axis=0, concat_axis=0, tiled=True)  23.8 us
    all_to_all x3, starting transfers between devices, swap(): return lax.all_to_all(x, axes, split_axis=0, concat_axis=0, tiled=True)  23.3 us
    pallas_call x5, Pallas kernels, vcall(): pl.pallas_call(kernel, out_shape=out, in_specs=specs, out_specs=outs, scr...  11.3 us
    unnamed x16, local copies, waits for them, and re-layouts  2.44 us
  transfers between devices with their start and end apart: 4, of which 4 were waited for; matrix products, arithmetic and copies ran while one was open for 0% of the time, Pallas kernels for 1%

profile of v1, /device:TPU:8, one launch (start us, length us, event | category | flops | bytes accessed | tf_op | source)
XLA Modules:
  0.0 100.2 jit_solution(12448690899657303212)
XLA Ops:
  0.0 0.9 copy-done.4
  0.9 1.0 shard_map.83
  1.9 14.8 %all-to-all-start.1 = ((bf16[16,16,128]{2,1,0:T(8,128)(2,1)}), bf16[16,16,128]{2,1,0:T(8,128)(2,1)S(1)}, u32[]{:S(2)}, u32[]{:S(2)}) async-start(bf16[16,16,128]{2,1,0:T(8,128)(2,1)} %shard_map.83), calls=%async_computation.1 | async-start | bytes 131072 | tf_op jit(solution)/shard_map/all_to_all | solution.py:178
  16.7 0.0 copy-start.5
  16.7 0.0 copy-start.6
  16.7 0.0 copy-done
  16.7 0.6 copy-done.5
  17.3 0.0 copy-done.6
  17.3 0.9 copy-done.3
  18.2 1.2 %shard_map.82 = bf16[8,192,128]{2,1,0:T(8,128)(2,1)} custom-call(bf16[128,512]{1,0:T(8,128)(2,1)S(1)} %copy-done.2, s32[1,128]{1,0:T(1,128)S(1)} %bitcast.6, s32[1,128]{1,0:T(1,128)S(1)} %bitcast.7, bf16[128,512]{1,0:T(8,128)(2,1)S(1)} %copy-done, bf16[512,128]{1,0:T(8,128)(2,1)S(1)} %copy-done.3), custom_call_target="tpu_custom_call" | custom-call | tf_op jit(solution)/shard_map/pallas_call | solution.py:163
  19.4 9.8 %all-to-all-done.1.pos_ref = bf16[16,16,128]{2,1,0:T(8,128)(2,1)S(1)} async-done(((bf16[16,16,128]{2,1,0:T(8,128)(2,1)}), bf16[16,16,128]{2,1,0:T(8,128)(2,1)S(1)}, u32[]{:S(2)}, u32[]{:S(2)}) %all-to-all-start.1) | async-done | bytes 65568 | tf_op jit(solution)/shard_map/all_to_all | solution.py:178
  29.3 5.2 %all-to-all-start = ((bf16[8,192,128]{2,1,0:T(8,128)(2,1)}), bf16[8,192,128]{2,1,0:T(8,128)(2,1)S(1)}, u32[]{:S(2)}, u32[]{:S(2)}) async-start(bf16[8,192,128]{2,1,0:T(8,128)(2,1)} %shard_map.82), calls=%async_computation | async-start | bytes 786432 | tf_op jit(solution)/shard_map/all_to_all | solution.py:178
  34.4 0.4 fusion
  34.9 8.8 %all-to-all-done.got_ref = bf16[8,192,128]{2,1,0:T(8,128)(2,1)S(1)} async-done(((bf16[8,192,128]{2,1,0:T(8,128)(2,1)}), bf16[8,192,128]{2,1,0:T(8,128)(2,1)S(1)}, u32[]{:S(2)}, u32[]{:S(2)}) %all-to-all-start) | async-done | bytes 393248 | tf_op jit(solution)/shard_map/all_to_all | solution.py:178
  43.6 0.2 shard_map.84
  43.9 23.6 %all_to_all.25.own_ref = bf16[8,2,128,128]{3,2,1,0:T(8,128)(2,1)S(1)} all-to-all(bf16[8,2,128,128]{3,2,1,0:T(8,128)(2,1)S(1)} %shard_map.84), channel_id=1, replica_groups=mesh['x'=4,'zh'=4,'zl'=2,'yh'=2,'c'=2,'head'=4] {'zh','yh'}, dimensions={0} | all-to-all | bytes 1048576 | tf_op jit(solution)/shard_map/all_to_all | solution.py:178
  67.5 1.9 %collective-permute-start = (bf16[8,2,128,128]{3,2,1,0:T(8,128)(2,1)S(1)}, bf16[8,2,128,128]{3,2,1,0:T(8,128)(2,1)S(1)}, u32[]{:S(2)}, u32[]{:S(2)}) collective-permute-start(bf16[8,2,128,128]{3,2,1,0:T(8,128)(2,1)S(1)} %all_to_all.25.own_ref), channel_id=1, source_target_pairs={{0,4},{4,0},{1,5},{5,1},{2,6},{6,2},{3,7},{7,3},{8,12},{12,8},{9,1... | collective-permute-start | bytes 1572872 | tf_op jit(solution)/shard_map/ppermute | solution.py:193
  69.4 1.9 %collective-permute-done.other_ref = bf16[8,2,128,128]{3,2,1,0:T(8,128)(2,1)S(1)} collective-permute-done((bf16[8,2,128,128]{3,2,1,0:T(8,128)(2,1)S(1)}, bf16[8,2,128,128]{3,2,1,0:T(8,128)(2,1)S(1)}, u32[]{:S(2)}, u32[]{:S(2)}) %collective-permute-start) | collective-permute-done | bytes 524320 | tf_op jit(solution)/shard_map/ppermute | solution.py:193
  71.3 7.7 %shard_map.85 = bf16[8,144,128]{2,1,0:T(8,128)(2,1)S(1)} custom-call(bf16[8,192,128]{2,1,0:T(8,128)(2,1)S(1)} %all-to-all-done.got_ref, bf16[8,2,128,128]{3,2,1,0:T(8,128)(2,1)S(1)} %all_to_all.25.own_ref, bf16[8,2,128,128]{3,2,1,0:T(8,128)(2,1)S(1)} %collective-permute-done.other_ref), custom_call_target="tpu_custom_call" | custom-call | tf_op jit(solution)/shard_map/pallas_call | solution.py:163
  79.0 10.9 %all_to_all.26.got_ref = bf16[8,144,128]{2,1,0:T(8,128)(2,1)S(1)} all-to-all(bf16[8,144,128]{2,1,0:T(8,128)(2,1)S(1)} %shard_map.85), channel_id=1, replica_groups=mesh['x'=4,'zh'=4,'zl'=2,'yh'=2,'c'=2,'head'=4] {'x','zl'}, dimensions={0} | all-to-all | bytes 589824 | tf_op jit(solution)/shard_map/all_to_all | solution.py:178
  89.9 1.1 %shard_map.86 = bf16[4,128,128]{2,1,0:T(8,128)(2,1)} custom-call(bf16[8,144,128]{2,1,0:T(8,128)(2,1)S(1)} %all_to_all.26.got_ref, bf16[128,512]{1,0:T(8,128)(2,1)S(1)} %copy-done.1), custom_call_target="tpu_custom_call" | custom-call | tf_op jit(solution)/shard_map/pallas_call | solution.py:163
  91.1 3.3 %all-to-all-start.4 = ((bf16[4,128,128]{2,1,0:T(8,128)(2,1)}), bf16[4,128,128]{2,1,0:T(8,128)(2,1)S(1)}, u32[]{:S(2)}, u32[]{:S(2)}) async-start(bf16[4,128,128]{2,1,0:T(8,128)(2,1)} %shard_map.86), calls=%async_computation.4 | async-start | bytes 262144 | tf_op jit(solution)/shard_map/all_to_all | solution.py:178
  94.4 5.1 %all-to-all-done.4 = bf16[4,128,128]{2,1,0:T(8,128)(2,1)S(1)} async-done(((bf16[4,128,128]{2,1,0:T(8,128)(2,1)}), bf16[4,128,128]{2,1,0:T(8,128)(2,1)S(1)}, u32[]{:S(2)}, u32[]{:S(2)}) %all-to-all-start.4) | async-done | bytes 131104 | tf_op jit(solution)/shard_map/all_to_all | solution.py:178
  99.6 0.6 add_convert_fusion
  (11 shorter events, 0.1 us)
Async XLA Ops:
  0.0 16.7 %copy-start = (bf16[128,512]{1,0:T(8,128)(2,1)S(1)}, bf16[128,512]{1,0:T(8,128)(2,1)}, u32[]{:S(2)}) copy-start(bf16[128,512]{1,0:T(8,128)(2,1)} %queries_ref.1) | copy-start | bytes 393220
  0.0 16.7 %copy-start.2 = (bf16[128,512]{1,0:T(8,128)(2,1)S(1)}, bf16[128,512]{1,0:T(8,128)(2,1)}, u32[]{:S(2)}) copy-start(bf16[128,512]{1,0:T(8,128)(2,1)} %source_ref.1) | copy-start | bytes 393220
  0.0 0.9 copy-start.4
  1.9 27.4 %all-to-all-start.1 = ((bf16[16,16,128]{2,1,0:T(8,128)(2,1)}), bf16[16,16,128]{2,1,0:T(8,128)(2,1)S(1)}, u32[]{:S(2)}, u32[]{:S(2)}) async-start(bf16[16,16,128]{2,1,0:T(8,128)(2,1)} %shard_map.83), calls=%async_computation.1 | async-start | bytes 131072 | tf_op jit(solution)/shard_map/all_to_all | solution.py:178
  16.7 0.7 copy-start.5
  16.7 0.7 copy-start.6
  17.3 0.9 copy-start.3
  19.4 15.0 %copy-start.7 = (bf16[512,2,128]{2,1,0:T(2,128)(2,1)S(1)}, bf16[512,2,128]{2,1,0:T(2,128)(2,1)}, u32[]{:S(2)}) copy-start(bf16[512,2,128]{2,1,0:T(2,128)(2,1)} %param.14) | copy-start | bytes 786436
  29.3 14.4 %all-to-all-start = ((bf16[8,192,128]{2,1,0:T(8,128)(2,1)}), bf16[8,192,128]{2,1,0:T(8,128)(2,1)S(1)}, u32[]{:S(2)}, u32[]{:S(2)}) async-start(bf16[8,192,128]{2,1,0:T(8,128)(2,1)} %shard_map.82), calls=%async_computation | async-start | bytes 786432 | tf_op jit(solution)/shard_map/all_to_all | solution.py:178
  67.5 3.8 %collective-permute-start = (bf16[8,2,128,128]{3,2,1,0:T(8,128)(2,1)S(1)}, bf16[8,2,128,128]{3,2,1,0:T(8,128)(2,1)S(1)}, u32[]{:S(2)}, u32[]{:S(2)}) collective-permute-start(bf16[8,2,128,128]{3,2,1,0:T(8,128)(2,1)S(1)} %all_to_all.25.own_ref), channel_id=1, source_target_pairs={{0,4},{4,0},{1,5},{5,1},{2,6},{6,2},{3,7},{7,3},{8,12},{12,8},{9,1... | collective-permute-start | bytes 1572872 | tf_op jit(solution)/shard_map/ppermute | solution.py:193
  79.0 10.9 %copy-start.1 = (bf16[128,512]{1,0:T(8,128)(2,1)S(1)}, bf16[128,512]{1,0:T(8,128)(2,1)}, u32[]{:S(2)}) copy-start(bf16[128,512]{1,0:T(8,128)(2,1)} %wo_ref.1) | copy-start | bytes 393220
  91.1 8.5 %all-to-all-start.4 = ((bf16[4,128,128]{2,1,0:T(8,128)(2,1)}), bf16[4,128,128]{2,1,0:T(8,128)(2,1)S(1)}, u32[]{:S(2)}, u32[]{:S(2)}) async-start(bf16[4,128,128]{2,1,0:T(8,128)(2,1)} %shard_map.86), calls=%async_computation.4 | async-start | bytes 262144 | tf_op jit(solution)/shard_map/all_to_all | solution.py:178

commit v2 on v1

--- a/solution.py
+++ b/solution.py
@@ -11,10 +11,12 @@
 HD = 64
 SPLIT = (("x", 4), ("zh", 4), ("zl", 2), ("yh", 2), ("c", 2))
 SEQ = tuple(n for n, _ in SPLIT)
-I = ("zh", "yh")
-J = ("x", "zl")
-NI = 8
-NJ = 8
+I = ("zl", "yh")
+J = ("x", "zh")
+NI = 4
+NJ = 16
+M = 2 * NI
+QAT = 4 * M
 BIG = 1048576.0
 CUT = 65536.0
 NEG = -1e30
@@ -47,19 +49,21 @@
     return lax.dot_general(a, b, (((ca,), (cb,)), ((), ())), preferred_element_type=F32)
 
 
-def split_kernel(pos_ref, out_ref):
-    row, col = iota((128, 128), 0), iota((128, 128), 1)
-    relay = onehot(col == seq_of(row // 16, row % 8, (row // 8) % 2))
-    for part in range(2):
-        out_ref[:, part * 8 : part * 8 + 8, :] = (
-            mm(relay, pos_ref[:, part, :]).astype(BF16).reshape(2 * NI, NJ, 128)
-        )
+def split_kernel(place_ref, own_ref, next_ref, keep_ref, send_ref):
+    zl, yh = place_ref[0], place_ref[1]
+    row, col = iota((64, 128), 0), iota((64, 128), 1)
+    for out_ref, half in ((keep_ref, yh), (send_ref, 1 - yh)):
+        b = seq_of(zl * 2 + half, (row // 2) % NJ, row % 2)
+        pick = [onehot((col == b) & (row // 32 == r)) for r in range(2)]
+        for part in range(2):
+            out = mm(pick[0], own_ref[:, part, :]) + mm(pick[1], next_ref[:, part, :])
+            out_ref[:, part * 128 : part * 128 + 128] = out.astype(BF16)
 
 
 def pack_kernel(source_ref, order_ref, avail_ref, queries_ref, wq_ref, out_ref):
     row, col = iota((128, 128), 0), iota((128, 128), 1)
     pick = onehot(jnp.broadcast_to(order_ref[...], (128, 128)) == row)
-    relay = onehot(row == seq_of((col // 2) % NI, col // 16, col % 2))
+    relay = onehot(row == seq_of((col // 2) % NI, col // M, col % 2))
     pick = mm(pick, relay).astype(BF16)
     avail = jnp.broadcast_to(avail_ref[...], (128, 128))
     diag = onehot((row == col) & (avail > 0))
@@ -70,21 +74,23 @@
     q = (q.astype(F32) * (2.0 / HD**0.5)).astype(BF16)
     for j in range(NJ):
         for part in range(4):
-            out_ref[j, part * 16 : part * 16 + 16, :] = rows[
-                j * 16 : j * 16 + 16, part * 128 : part * 128 + 128
+            out_ref[j, part * M : part * M + M, :] = rows[
+                j * M : j * M + M, part * 128 : part * 128 + 128
             ]
-        out_ref[j, 64:192, :] = q
-
-
-def project_kernel(got_ref, pos_ref, wk_ref, wv_ref, out_ref):
-    parts = [got_ref[:, part * 16 : part * 16 + 16, :].reshape(128, 128) for part in range(4)]
+        out_ref[j, QAT : QAT + 128, :] = q
+
+
+def project_kernel(place_ref, got_ref, pos_ref, wk_ref, wv_ref, out_ref):
+    parts = [got_ref[:, part * M : part * M + M, :].reshape(128, 128) for part in range(4)]
     live = parts[0].astype(F32) < CUT
     rows = jnp.concatenate(parts, axis=1)
-    row, col = iota((128, 128), 0), iota((128, 128), 1)
-    relay = onehot(col == (row % 16) * 8 + row // 16)
+    zl, yh, c = place_ref[0], place_ref[1], place_ref[2]
+    row, col = iota((128, 256), 0), iota((128, 256), 1)
+    near = (((row // 2) % 2) ^ yh) * 64 + (((row // 4) % 2) ^ zl) * 32
+    relay = onehot(col == (row % 2) * 128 + near + (row // M) * 2 + c)
+    pos = mm(relay, pos_ref[...])
     for part, w_ref, mark in ((0, wk_ref, BIG), (1, wv_ref, 0.0)):
-        pos = pos_ref[:, part * 8 : part * 8 + 8, :].reshape(128, 128)
-        out = mm(rows, w_ref[...]) + mm(relay, pos)
+        out = mm(rows, w_ref[...]) + pos[:, part * 128 : part * 128 + 128]
         out = jnp.where(live, out, F32(mark)).astype(BF16)
         for i in range(NI):
             out_ref[i, part] = out
@@ -111,7 +117,7 @@
     per = qb // 128
 
     def block(t, carry):
-        q = got_ref[pl.ds(t * per, per), 64:192, :].reshape(qb, 128).astype(F32)
+        q = got_ref[pl.ds(t * per, per), QAT : QAT + 128, :].reshape(qb, 128).astype(F32)
         sums, tops = [], []
         for h in range(2):
             mine = (lane >= 64) if h else (lane < 64)
@@ -179,23 +185,33 @@
 
 
 def local(queries, source, order, avail, pos_table, w_query, w_keyval, w_out):
-    pos = swap(vcall(split_kernel, bf(2 * NI, 16, 128), (pos_table,)), (*I, "c"))
+    place = jnp.stack([lax.axis_index(n).astype(jnp.int32) for n in ("zl", "yh", "c")])
+    pair = ((0, 1), (1, 0))
+    following = lax.ppermute(pos_table, "zl", pair)
+    keep, send = vcall(
+        split_kernel, (bf(64, 256), bf(64, 256)), (place, pos_table, following), 1
+    )
+    pos = jnp.concatenate([keep, lax.ppermute(send, "yh", pair)], axis=0)
+    pos = lax.all_gather(pos, "c", axis=0, tiled=True)
     packed = vcall(
         pack_kernel,
-        bf(NJ, 192, 128),
+        bf(NJ, QAT + 128, 128),
         (source, order.reshape(1, 128), avail.reshape(1, 128), queries, w_query),
     )
     got = swap(packed, J)
     spread = vcall(
-        project_kernel, bf(NI, 2, 128, 128), (got, pos, w_keyval[:, 0], w_keyval[:, 1])
+        project_kernel,
+        bf(NI, 2, 128, 128),
+        (place, got, pos, w_keyval[:, 0], w_keyval[:, 1]),
+        1,
     )
     own = swap(spread, I)
-    other = lax.ppermute(own, "c", ((0, 1), (1, 0)))
+    other = lax.ppermute(own, "c", pair)
     partial = vcall(
         functools.partial(attend_kernel, qb=256),
         bf(NJ, 144, 128),
         (got, own, other),
-        scratch=(pltpu.VMEM((2, 2048, 128), BF16), pltpu.VMEM((2, 2048, 128), BF16)),
+        scratch=(pltpu.VMEM((2, 1024, 128), BF16), pltpu.VMEM((2, 1024, 128), BF16)),
     )
     partial = swap(partial, J)
     terms = vcall(combine_kernel, bf(4, 128, 128), (partial, w_out))

time: 101 us -> 124 us (1.23)
  blocking collectives: 34.5 us -> 51.2 us
  Pallas kernels: 11.3 us -> 15.3 us
  starting transfers between devices: 25.2 us -> 28.5 us
  waiting for transfers between devices: 25.6 us -> 22.8 us
    all_to_all x3 -> x2, waiting for transfers between devices: 23.8 us -> 5.17 us  [swap(): return lax.all_to_all(x, axes, split_axis=0, concat_axis=0, tiled=True)]
    ppermute x1 -> x3, waiting for transfers between devices: 1.88 us -> 17.6 us  [the longest x1 13.2 us: local(): following = lax.ppermute(pos_table, 'zl', pair)]
    all_to_all x2, blocking collectives: 34.5 us -> 49.3 us  [swap(): return lax.all_to_all(x, axes, split_axis=0, concat_axis=0, tiled=True)]
    ppermute x1 -> x3, starting transfers between devices: 1.91 us -> 12.1 us  [the longest x1 6.84 us: local(): pos = jnp.concatenate([keep, lax.ppermute(send, 'yh', pair)], axis=0)]
    all_to_all x3 -> x2, starting transfers between devices: 23.3 us -> 16.4 us  [swap(): return lax.all_to_all(x, axes, split_axis=0, concat_axis=0, tiled=True)]
    pallas_call x5, Pallas kernels: 11.3 us -> 15.3 us  [vcall(): pl.pallas_call(kernel, out_shape=out, in_specs=specs, out_specs=outs, scr...]
    all_gather x0 -> x1, blocking collectives: none -> 1.89 us  [local(): pos = lax.all_gather(pos, 'c', axis=0, tiled=True)]
  transfers between devices with their start and end apart: 4 -> 5, of which waited for: 4 -> 4; matrix products, arithmetic and copies ran while one was open for 0% -> 0% of each run, Pallas kernels for 1% -> 1%
where the time goes in v2:
time: 124 us; the launch traced here: 123 us
  blocking collectives  51.2 us (41%)
  starting transfers between devices  28.5 us (23%)
  waiting for transfers between devices  22.8 us (18%)
  Pallas kernels  15.3 us (12%)
  local copies, waits for them, and re-layouts  3.8 us (3%)
  other arithmetic  1.49 us (1%)
    all_to_all x2, blocking collectives, swap(): return lax.all_to_all(x, axes, split_axis=0, concat_axis=0, tiled=True)  49.3 us
    all_to_all x2, starting transfers between devices, swap(): return lax.all_to_all(x, axes, split_axis=0, concat_axis=0, tiled=True)  16.4 us
    pallas_call x5, Pallas kernels, vcall(): pl.pallas_call(kernel, out_shape=out, in_specs=specs, out_specs=outs, scr...  15.3 us
    ppermute x1, waiting for transfers between devices, local(): following = lax.ppermute(pos_table, 'zl', pair)  13.2 us
    ppermute x1, starting transfers between devices, local(): pos = jnp.concatenate([keep, lax.ppermute(send, 'yh', pair)], axis=0)  6.84 us
    all_to_all x2, waiting for transfers between devices, swap(): return lax.all_to_all(x, axes, split_axis=0, concat_axis=0, tiled=True)  5.17 us
    unnamed x16, local copies, waits for them, and re-layouts  3.39 us
    ppermute x1, starting transfers between devices, local(): following = lax.ppermute(pos_table, 'zl', pair)  3.38 us
  transfers between devices with their start and end apart: 5, of which 4 were waited for; matrix products, arithmetic and copies ran while one was open for 0% of the time, Pallas kernels for 1%

profile of v2, /device:TPU:8, one launch (start us, length us, event | category | flops | bytes accessed | tf_op | source)
XLA Modules:
  0.0 123.2 jit_solution(8283041567796649598)
XLA Ops:
  0.0 0.7 copy-done.5
  0.7 0.9 copy-done
  1.6 0.9 copy-done.1
  2.5 0.9 copy-done.2
  3.4 1.3 %shard_map.82 = bf16[16,160,128]{2,1,0:T(8,128)(2,1)} custom-call(bf16[128,512]{1,0:T(8,128)(2,1)S(1)} %copy-done.1, s32[1,128]{1,0:T(1,128)S(1)} %bitcast.9, s32[1,128]{1,0:T(1,128)S(1)} %bitcast.10, bf16[128,512]{1,0:T(8,128)(2,1)S(1)} %copy-done, bf16[512,128]{1,0:T(8,128)(2,1)S(1)} %copy-done.2), custom_call_target="tpu_custom_call" | custom-call | tf_op jit(solution)/shard_map/pallas_call | solution.py:169
  4.7 13.0 %all-to-all-start = ((bf16[16,160,128]{2,1,0:T(8,128)(2,1)}), bf16[16,160,128]{2,1,0:T(8,128)(2,1)S(1)}, u32[]{:S(2)}, u32[]{:S(2)}) async-start(bf16[16,160,128]{2,1,0:T(8,128)(2,1)} %shard_map.82), calls=%async_computation | async-start | bytes 1310720 | tf_op jit(solution)/shard_map/all_to_all | solution.py:184
  17.7 3.4 %collective-permute-start = (bf16[128,2,128]{2,1,0:T(2,128)(2,1)S(1)}, bf16[128,2,128]{2,1,0:T(2,128)(2,1)S(1)}, u32[]{:S(2)}, u32[]{:S(2)}) collective-permute-start(bf16[128,2,128]{2,1,0:T(2,128)(2,1)S(1)} %copy-done.4), channel_id=1, source_target_pairs={{0,16},{16,0},{1,17},{17,1},{2,18},{18,2},{3,19},{19,3},{4,20},{20... | collective-permute-start | bytes 196616 | tf_op jit(solution)/shard_map/ppermute | solution.py:190
  21.1 0.4 fusion
  21.5 0.1 pad_add_fusion.place_ref
  21.6 13.2 %collective-permute-done.next_ref = bf16[128,2,128]{2,1,0:T(2,128)(2,1)S(1)} collective-permute-done((bf16[128,2,128]{2,1,0:T(2,128)(2,1)S(1)}, bf16[128,2,128]{2,1,0:T(2,128)(2,1)S(1)}, u32[]{:S(2)}, u32[]{:S(2)}) %collective-permute-start) | collective-permute-done | bytes 65568 | tf_op jit(solution)/shard_map/ppermute | solution.py:190
  34.8 1.3 %shard_map.83 = (bf16[64,256]{1,0:T(8,128)(2,1)S(1)}, bf16[64,256]{1,0:T(8,128)(2,1)S(1)}) custom-call(s32[3]{0:T(128)S(1)} %pad_add_fusion.place_ref, bf16[128,2,128]{2,1,0:T(2,128)(2,1)S(1)} %copy-done.4, bf16[128,2,128]{2,1,0:T(2,128)(2,1)S(1)} %collective-permute-done.next_ref), custom_call_target="tpu_custom_call" | custom-call | tf_op jit(solution)/shard_map/pallas_call | solution.py:169
  36.0 6.8 %collective-permute-start.1 = (bf16[64,256]{1,0:T(8,128)(2,1)S(1)}, bf16[64,256]{1,0:T(8,128)(2,1)S(1)}, u32[]{:S(2)}, u32[]{:S(2)}) collective-permute-start(bf16[64,256]{1,0:T(8,128)(2,1)S(1)} %get-tuple-element.8), channel_id=1, source_target_pairs={{0,8},{8,0},{1,9},{9,1},{2,10},{10,2},{3,11},{11,3},{4,12},{12,4},... | collective-permute-start | bytes 98312 | tf_op jit(solution)/shard_map/ppermute | solution.py:194
  42.9 3.0 %collective-permute-done.1 = bf16[64,256]{1,0:T(8,128)(2,1)S(1)} collective-permute-done((bf16[64,256]{1,0:T(8,128)(2,1)S(1)}, bf16[64,256]{1,0:T(8,128)(2,1)S(1)}, u32[]{:S(2)}, u32[]{:S(2)}) %collective-permute-start.1) | collective-permute-done | bytes 32800 | tf_op jit(solution)/shard_map/ppermute | solution.py:194
  45.9 1.9 %all_gather.3.pos_ref = bf16[256,256]{1,0:T(8,128)(2,1)S(1)} all-gather(bf16[128,256]{1,0:T(8,128)(2,1)S(1)} %pad_maximum_fusion), channel_id=1, replica_groups=mesh['x'=4,'zh'=4,'zl'=2,'yh'=2,'c'=2,'head'=4] {'c'}, dimensions={0}, use_global_device_ids=true | all-gather | bytes 196608 | tf_op jit(solution)/shard_map/all_gather | solution.py:195
  47.8 0.8 shard_map.84
  48.6 18.7 %all_to_all.20.own_ref = bf16[4,2,128,128]{3,2,1,0:T(8,128)(2,1)S(1)} all-to-all(bf16[4,2,128,128]{3,2,1,0:T(8,128)(2,1)S(1)} %shard_map.84), channel_id=1, replica_groups=mesh['x'=4,'zh'=4,'zl'=2,'yh'=2,'c'=2,'head'=4] {'zl','yh'}, dimensions={0} | all-to-all | bytes 524288 | tf_op jit(solution)/shard_map/all_to_all | solution.py:184
  67.3 1.9 %collective-permute-start.2 = (bf16[4,2,128,128]{3,2,1,0:T(8,128)(2,1)S(1)}, bf16[4,2,128,128]{3,2,1,0:T(8,128)(2,1)S(1)}, u32[]{:S(2)}, u32[]{:S(2)}) collective-permute-start(bf16[4,2,128,128]{3,2,1,0:T(8,128)(2,1)S(1)} %all_to_all.20.own_ref), channel_id=1, source_target_pairs={{0,4},{4,0},{1,5},{5,1},{2,6},{6,2},{3,7},{7,3},{8,12},{12,8},{9,1... | collective-permute-start | bytes 786440 | tf_op jit(solution)/shard_map/ppermute | solution.py:209
  69.2 1.5 %collective-permute-done.2.other_ref = bf16[4,2,128,128]{3,2,1,0:T(8,128)(2,1)S(1)} collective-permute-done((bf16[4,2,128,128]{3,2,1,0:T(8,128)(2,1)S(1)}, bf16[4,2,128,128]{3,2,1,0:T(8,128)(2,1)S(1)}, u32[]{:S(2)}, u32[]{:S(2)}) %collective-permute-start.2) | collective-permute-done | bytes 262176 | tf_op jit(solution)/shard_map/ppermute | solution.py:209
  70.7 10.6 %shard_map.85 = bf16[16,144,128]{2,1,0:T(8,128)(2,1)S(1)} custom-call(bf16[16,160,128]{2,1,0:T(8,128)(2,1)S(1)} %all-to-all-done.got_ref, bf16[4,2,128,128]{3,2,1,0:T(8,128)(2,1)S(1)} %all_to_all.20.own_ref, bf16[4,2,128,128]{3,2,1,0:T(8,128)(2,1)S(1)} %collective-permute-done.2.other_ref), custom_call_target="tpu_custom_call" | custom-call | tf_op jit(solution)/shard_map/pallas_call | solution.py:169
  81.3 30.6 %all_to_all.21.got_ref = bf16[16,144,128]{2,1,0:T(8,128)(2,1)S(1)} all-to-all(bf16[16,144,128]{2,1,0:T(8,128)(2,1)S(1)} %shard_map.85), channel_id=1, replica_groups=mesh['x'=4,'zh'=4,'zl'=2,'yh'=2,'c'=2,'head'=4] {'x','zh'}, dimensions={0} | all-to-all | bytes 1179648 | tf_op jit(solution)/shard_map/all_to_all | solution.py:184
  111.9 1.3 %shard_map.86 = bf16[4,128,128]{2,1,0:T(8,128)(2,1)} custom-call(bf16[16,144,128]{2,1,0:T(8,128)(2,1)S(1)} %all_to_all.21.got_ref, bf16[128,512]{1,0:T(8,128)(2,1)S(1)} %copy-done.3), custom_call_target="tpu_custom_call" | custom-call | tf_op jit(solution)/shard_map/pallas_call | solution.py:169
  113.2 3.4 %all-to-all-start.3 = ((bf16[4,128,128]{2,1,0:T(8,128)(2,1)}), bf16[4,128,128]{2,1,0:T(8,128)(2,1)S(1)}, u32[]{:S(2)}, u32[]{:S(2)}) async-start(bf16[4,128,128]{2,1,0:T(8,128)(2,1)} %shard_map.86), calls=%async_computation.3 | async-start | bytes 262144 | tf_op jit(solution)/shard_map/all_to_all | solution.py:184
  116.6 5.2 %all-to-all-done.3 = bf16[4,128,128]{2,1,0:T(8,128)(2,1)S(1)} async-done(((bf16[4,128,128]{2,1,0:T(8,128)(2,1)}), bf16[4,128,128]{2,1,0:T(8,128)(2,1)S(1)}, u32[]{:S(2)}, u32[]{:S(2)}) %all-to-all-start.3) | async-done | bytes 131104 | tf_op jit(solution)/shard_map/all_to_all | solution.py:184
  121.8 1.4 %add_convert_fusion = bf16[128,128]{1,0:T(8,128)(2,1)} fusion(f32[128,128]{1,0:T(8,128)S(1)} %convert_reduce_fusion, bf16[128,512]{1,0:T(8,128)(2,1)} %queries_ref.1, s32[]{:T(128)S(6)} %select_n.3), kind=kLoop, calls=%fused_computation.4 | loop fusion | flops 49152 | bytes 131076 | tf_op jit(solution)/shard_map/convert_element_type | solution.py:220
  (16 shorter events, 0.1 us)
Async XLA Ops:
  0.0 0.7 copy-start.5
  0.0 0.7 copy-start.6
  0.7 0.9 copy-start
  1.6 0.9 copy-start.1
  2.5 0.9 copy-start.2
  4.7 13.0 %copy-start.4 = (bf16[128,2,128]{2,1,0:T(2,128)(2,1)S(1)}, bf16[128,2,128]{2,1,0:T(2,128)(2,1)}, u32[]{:S(2)}) copy-start(bf16[128,2,128]{2,1,0:T(2,128)(2,1)} %own_ref.1) | copy-start | bytes 196612
  4.7 16.4 %copy-start.7 = (bf16[512,2,128]{2,1,0:T(2,128)(2,1)S(1)}, bf16[512,2,128]{2,1,0:T(2,128)(2,1)}, u32[]{:S(2)}) copy-start(bf16[512,2,128]{2,1,0:T(2,128)(2,1)} %param.14) | copy-start | bytes 786436
  4.7 43.1 %all-to-all-start = ((bf16[16,160,128]{2,1,0:T(8,128)(2,1)}), bf16[16,160,128]{2,1,0:T(8,128)(2,1)S(1)}, u32[]{:S(2)}, u32[]{:S(2)}) async-start(bf16[16,160,128]{2,1,0:T(8,128)(2,1)} %shard_map.82), calls=%async_computation | async-start | bytes 1310720 | tf_op jit(solution)/shard_map/all_to_all | solution.py:184
  17.7 17.0 %collective-permute-start = (bf16[128,2,128]{2,1,0:T(2,128)(2,1)S(1)}, bf16[128,2,128]{2,1,0:T(2,128)(2,1)S(1)}, u32[]{:S(2)}, u32[]{:S(2)}) collective-permute-start(bf16[128,2,128]{2,1,0:T(2,128)(2,1)S(1)} %copy-done.4), channel_id=1, source_target_pairs={{0,16},{16,0},{1,17},{17,1},{2,18},{18,2},{3,19},{19,3},{4,20},{20... | collective-permute-start | bytes 196616 | tf_op jit(solution)/shard_map/ppermute | solution.py:190
  36.0 9.9 %collective-permute-start.1 = (bf16[64,256]{1,0:T(8,128)(2,1)S(1)}, bf16[64,256]{1,0:T(8,128)(2,1)S(1)}, u32[]{:S(2)}, u32[]{:S(2)}) collective-permute-start(bf16[64,256]{1,0:T(8,128)(2,1)S(1)} %get-tuple-element.8), channel_id=1, source_target_pairs={{0,8},{8,0},{1,9},{9,1},{2,10},{10,2},{3,11},{11,3},{4,12},{12,4},... | collective-permute-start | bytes 98312 | tf_op jit(solution)/shard_map/ppermute | solution.py:194
  67.3 3.4 %collective-permute-start.2 = (bf16[4,2,128,128]{3,2,1,0:T(8,128)(2,1)S(1)}, bf16[4,2,128,128]{3,2,1,0:T(8,128)(2,1)S(1)}, u32[]{:S(2)}, u32[]{:S(2)}) collective-permute-start(bf16[4,2,128,128]{3,2,1,0:T(8,128)(2,1)S(1)} %all_to_all.20.own_ref), channel_id=1, source_target_pairs={{0,4},{4,0},{1,5},{5,1},{2,6},{6,2},{3,7},{7,3},{8,12},{12,8},{9,1... | collective-permute-start | bytes 786440 | tf_op jit(solution)/shard_map/ppermute | solution.py:209
  81.3 30.6 %copy-start.3 = (bf16[128,512]{1,0:T(8,128)(2,1)S(1)}, bf16[128,512]{1,0:T(8,128)(2,1)}, u32[]{:S(2)}) copy-start(bf16[128,512]{1,0:T(8,128)(2,1)} %wo_ref.1) | copy-start | bytes 393220
  113.2 8.5 %all-to-all-start.3 = ((bf16[4,128,128]{2,1,0:T(8,128)(2,1)}), bf16[4,128,128]{2,1,0:T(8,128)(2,1)S(1)}, u32[]{:S(2)}, u32[]{:S(2)}) async-start(bf16[4,128,128]{2,1,0:T(8,128)(2,1)} %shard_map.86), calls=%async_computation.3 | async-start | bytes 262144 | tf_op jit(solution)/shard_map/all_to_all | solution.py:184
